TPU v7x, 32 devices: a whole 2x2x4 slice. The times are simulated.
32 devices in a mesh: row: 8 (over y, x, core), col: 4 (over z).
Axes of the slice: x: 2, y: 2, z: 4, core: 2. Of those that a mesh axis runs over, the one named last changes fastest.
Arguments:
- matrix: float32 [8, 3, 256, 4, 6, 256], P('row', None, None, 'col'), as said below
- checksum: float32 [8, 3, 256, 6, 256], P('row'), as said below
- failed: int32 [4], P('col'), may hold values from 0 to 3, as said below
Outputs:
- factored: float32 [8, 3, 256, 4, 6, 256], P('row', None, None, 'col')
- updated_checksum_result: float32 [8, 3, 256, 6, 256], P('row')
Inputs may be any that keep to these rules, and one draw needn't show every extreme that they name: `failed`: a permutation of the grid column indices; entry 0 names the grid column whose tiles in matrix carry no information. With the lost grid column rebuilt from checksum, matrix is symmetric positive definite. `checksum`: for each grid row, the sum over all grid columns of the intact matrix's tiles, the lost column included.
All inputs are finite; a program needn't handle non-finite values.
Results may differ from a plain program's by a relative error of at most 0.0003.
Values sent between devices are 32-bit elements; how exact they have to be, the bound alone decides.
A program may use at most 128 MiB of HBM per device.

v0:
```python
import jax
import jax.numpy as jnp
from jax import lax
from jax.sharding import PartitionSpec as P

PANELS = 3


def spread_2(block, axis, holder):
    block = jnp.where(lax.axis_index(axis) == holder, block, jnp.zeros_like(block))
    return lax.psum(block, axis)


def solve_panel(column, factor, row_tiles, panel):
    tile_count, width = (column.shape[0], column.shape[1])
    stacked = column.reshape(tile_count * width, width)
    solved = jax.scipy.linalg.solve_triangular(factor, stacked.T, lower=True).T.reshape(
        tile_count, width, width
    )
    chosen = jnp.where((row_tiles > panel)[:, None, None], solved, 0.0)
    return jnp.where((row_tiles == panel)[:, None, None], factor[None, :, :], chosen)


def matching_tiles(panel_rows, column_position, rows_count, cols_count):
    width = panel_rows.shape[1]
    repeats = max(rows_count // cols_count, 1)
    received = []
    for offset in range(repeats):
        source = (column_position + offset * cols_count) % rows_count
        received.append(spread_2(panel_rows, "row", source))
    return jnp.stack(received, axis=1).reshape(-1, width, width)


def shards(matrix, checksum, failed):
    rows_count = lax.axis_size("row")
    cols_count = lax.axis_size("col")
    row_index = lax.axis_index("row")
    column_position = lax.axis_index("col")
    tile_rows, width, tile_cols = (matrix.shape[1], matrix.shape[2], matrix.shape[4])
    resident_tiles = matrix.reshape(tile_rows, width, tile_cols, width)
    totals = checksum.reshape(tile_rows, width, tile_cols, width)
    missing_tiles = lax.all_gather(failed, "col", axis=0, tiled=True)[0]
    healthy_member = jnp.where(column_position != missing_tiles, resident_tiles, 0.0)
    remaining_peers = lax.psum(healthy_member, "col")
    work = jnp.where(column_position == missing_tiles, totals - remaining_peers, resident_tiles)
    row_tiles = row_index + jnp.arange(tile_rows, dtype=jnp.int32) * rows_count
    col_tiles = column_position + jnp.arange(tile_cols, dtype=jnp.int32) * cols_count
    identity = jnp.eye(width, dtype=jnp.float32)
    finished = []
    for panel in range(PANELS):
        col_root = panel % cols_count
        col_slot = panel // cols_count
        row_root = panel % rows_count
        row_slot = panel // rows_count
        column = work[:, :, col_slot, :]
        owner = jnp.logical_and(row_index == row_root, column_position == col_root)
        diag_input = jnp.where(owner, work[row_slot, :, col_slot, :], identity)
        factor_here = jnp.linalg.cholesky(diag_input)
        factor = spread_2(factor_here, "row", row_root)
        own_rows = solve_panel(column, factor, row_tiles, panel)
        panel_rows = spread_2(own_rows, "col", col_root)
        panel_cols = matching_tiles(panel_rows, column_position, rows_count, cols_count)
        update = jnp.einsum(
            "axr,byr->axby", panel_rows, panel_cols, precision=lax.Precision.HIGHEST
        )
        work = work - update
        finished.append((col_root, col_slot, panel_rows))
    totals = lax.psum(work, "col")
    for col_root, col_slot, panel_rows in finished:
        current = work[:, :, col_slot, :]
        work = work.at[:, :, col_slot, :].set(
            jnp.where(column_position == col_root, panel_rows, current)
        )
    keep = (row_tiles[:, None] >= col_tiles[None, :])[:, None, :, None]
    factored = jnp.where(keep, work, 0.0).reshape(matrix.shape)
    return (factored, totals.reshape(checksum.shape))


def solution(mesh):
    return jax.shard_map(
        shards,
        mesh=mesh,
        in_specs=(
            P("row", None, None, "col", None, None),
            P("row", None, None, None, None),
            P("col"),
        ),
        out_specs=(P("row", None, None, "col", None, None), P("row", None, None, None, None)),
        check_vma=False,
    )
```

profile of v0, /device:TPU:0, one launch (start us, length us, event | category | flops | bytes accessed | tf_op | source)
XLA Modules:
  0.0 1121.8 jit_solution(12888516157622875369)
XLA Ops:
  7.9 1.2 dynamic-slice.31
  9.9 9.9 all-reduce.1
  19.8 12.1 %copy.25 = f32[1,3,256,1,6,256]{2,5,4,1,3,0:T(8,128)} copy(f32[1,3,256,1,6,256]{5,3,4,2,1,0:T(1,128)} %param.12) | data formatting | bytes 9437184 | tf_op args[0]
  31.9 5.0 bitcast_select_fusion.1
  37.0 6.1 copy.24
  43.1 165.1 %all-reduce.17.cloned.1.call-done = f32[3,256,6,256]{1,3,2,0:T(8,128)} async-done(((f32[3,256,6,256]{1,3,2,0:T(8,128)}), f32[3,256,6,256]{1,3,2,0:T(8,128)}) %all-reduce.17.cloned.1.call-update) | async-done | bytes 4718608 | tf_op jit(solution)/shard_map/psum | solution.py:44
  208.2 6.3 bitcast_select_fusion
  214.5 2.2 copy-done.1
  216.9 1.1 fusion.12
  217.9 11.7 %cholesky.172 = f32[128,128]{1,0:T(8,128)S(1)} custom-call(f32[128,128]{1,0:T(8,128)S(1)} %cholesky.270), custom_call_target="Cholesky" | custom-call | tf_op jit(solution)/shard_map/jit(cholesky)/cholesky | solution.py:58
  229.7 9.8 custom-call.15
  240.0 11.7 %cholesky.189 = f32[128,128]{1,0:T(8,128)S(1)} custom-call(f32[128,128]{1,0:T(8,128)S(1)} %convolution_subtract_fusion.8), custom_call_target="Cholesky" | custom-call | tf_op jit(solution)/shard_map/jit(cholesky)/cholesky | solution.py:58
  255.1 52.3 %all-reduce.19.cloned.1.call-done = f32[256,256]{1,0:T(8,128)} async-done(((f32[256,256]{1,0:T(8,128)}), f32[256,256]{1,0:T(8,128)}) %all-reduce.19.cloned.1.call-update) | async-done | bytes 262160 | tf_op jit(solution)/shard_map/psum | solution.py:11
  308.5 4.0 while.9
  309.1 1.4 bitcast_dynamic-update-slice_fusion.9
  311.1 1.4 bitcast_dynamic-update-slice_fusion.9
  312.5 19.7 %custom-call.16 = f32[2,128,128]{1,2,0:T(8,128)S(1)} custom-call(f32[2,128,128]{2,1,0:T(8,128)S(1)} %get-tuple-element.60), custom_call_target="InvertDiagBlocksLowerTriangular" | custom-call | tf_op jit(solution)/shard_map/jit(_solve_triangular)/triangular_solve | solution.py:17
  334.8 1.0 select_select_fusion.2
  335.9 43.3 %all-reduce.21.cloned.1.call-done = f32[3,256,256]{1,2,0:T(8,128)} async-done(((f32[3,256,256]{1,2,0:T(8,128)}), f32[3,256,256]{1,2,0:T(8,128)}) %all-reduce.21.cloned.1.call-update) | async-done | bytes 786448 | tf_op jit(solution)/shard_map/psum | solution.py:11
  379.3 2.5 select_bitcast_fusion.6
  381.8 59.4 %all-reduce.37.cloned.1.call-done = (f32[3,1,256,256]{2,3,0,1:T(8,128)}, f32[3,1,256,256]{2,3,0,1:T(8,128)}) async-done(((f32[3,1,256,256]{2,3,0,1:T(8,128)}, f32[3,1,256,256]{2,3,0,1:T(8,128)}), (f32[3,1,256,256]{2,3,0,1:T(8,128)}, f32[3,1,256,256]{2,3,0,1:T(8,128)})) %all-reduce.37.cloned.1.call-update) | async-done | bytes 1572880 | tf_op jit(solution)/shard_map/psum | solution.py:11
  441.2 1.5 pad_maximum_fusion
  442.7 1.6 copy.31
  444.3 7.3 convolution_subtract_fusion.2
  451.7 2.2 copy-done.2
  454.0 1.1 fusion.11
  455.1 11.7 %cholesky.206 = f32[128,128]{1,0:T(8,128)S(1)} custom-call(f32[128,128]{1,0:T(8,128)S(1)} %cholesky.273), custom_call_target="Cholesky" | custom-call | tf_op jit(solution)/shard_map/jit(cholesky)/cholesky | solution.py:58
  467.5 9.8 custom-call.17
  477.8 11.9 %cholesky.223 = f32[128,128]{1,0:T(8,128)S(1)} custom-call(f32[128,128]{1,0:T(8,128)S(1)} %convolution_subtract_fusion.7), custom_call_target="Cholesky" | custom-call | tf_op jit(solution)/shard_map/jit(cholesky)/cholesky | solution.py:58
  492.7 52.9 %all-reduce.23.cloned.1.call-done = f32[256,256]{1,0:T(8,128)} async-done(((f32[256,256]{1,0:T(8,128)}), f32[256,256]{1,0:T(8,128)}) %all-reduce.23.cloned.1.call-update) | async-done | bytes 262160 | tf_op jit(solution)/shard_map/psum | solution.py:11
  546.6 4.0 while.10
  547.2 1.4 bitcast_dynamic-update-slice_fusion.10
  549.2 1.4 bitcast_dynamic-update-slice_fusion.10
  550.6 19.7 %custom-call.18 = f32[2,128,128]{1,2,0:T(8,128)S(1)} custom-call(f32[2,128,128]{2,1,0:T(8,128)S(1)} %get-tuple-element.61), custom_call_target="InvertDiagBlocksLowerTriangular" | custom-call | tf_op jit(solution)/shard_map/jit(_solve_triangular)/triangular_solve | solution.py:17
  572.9 1.0 select_select_fusion.1
  574.0 43.4 %all-reduce.25.cloned.1.call-done = f32[3,256,256]{1,2,0:T(8,128)} async-done(((f32[3,256,256]{1,2,0:T(8,128)}), f32[3,256,256]{1,2,0:T(8,128)}) %all-reduce.25.cloned.1.call-update) | async-done | bytes 786448 | tf_op jit(solution)/shard_map/psum | solution.py:11
  617.4 2.5 select_bitcast_fusion.4
  620.2 59.3 %all-reduce.35.cloned.1.call-done = (f32[3,1,256,256]{2,3,0,1:T(8,128)}, f32[3,1,256,256]{2,3,0,1:T(8,128)}) async-done(((f32[3,1,256,256]{2,3,0,1:T(8,128)}, f32[3,1,256,256]{2,3,0,1:T(8,128)}), (f32[3,1,256,256]{2,3,0,1:T(8,128)}, f32[3,1,256,256]{2,3,0,1:T(8,128)})) %all-reduce.35.cloned.1.call-update) | async-done | bytes 1572880 | tf_op jit(solution)/shard_map/psum | solution.py:11
  679.5 2.7 pad_maximum_fusion.1
  682.2 3.0 copy.39
  685.2 7.3 convolution_subtract_fusion.1
  692.6 2.2 copy-done.3
  694.9 1.1 fusion.10
  696.0 11.7 %cholesky.240 = f32[128,128]{1,0:T(8,128)S(1)} custom-call(f32[128,128]{1,0:T(8,128)S(1)} %cholesky.276), custom_call_target="Cholesky" | custom-call | tf_op jit(solution)/shard_map/jit(cholesky)/cholesky | solution.py:58
  708.4 9.8 custom-call.19
  718.7 11.9 %cholesky.257 = f32[128,128]{1,0:T(8,128)S(1)} custom-call(f32[128,128]{1,0:T(8,128)S(1)} %convolution_subtract_fusion.6), custom_call_target="Cholesky" | custom-call | tf_op jit(solution)/shard_map/jit(cholesky)/cholesky | solution.py:58
  733.7 52.9 %all-reduce.27.cloned.1.call-done = f32[256,256]{1,0:T(8,128)} async-done(((f32[256,256]{1,0:T(8,128)}), f32[256,256]{1,0:T(8,128)}) %all-reduce.27.cloned.1.call-update) | async-done | bytes 262160 | tf_op jit(solution)/shard_map/psum | solution.py:11
  787.6 4.0 while.11
  788.3 1.4 bitcast_dynamic-update-slice_fusion.11
  790.2 1.4 bitcast_dynamic-update-slice_fusion.11
  791.6 19.7 %custom-call.20 = f32[2,128,128]{1,2,0:T(8,128)S(1)} custom-call(f32[2,128,128]{2,1,0:T(8,128)S(1)} %get-tuple-element.62), custom_call_target="InvertDiagBlocksLowerTriangular" | custom-call | tf_op jit(solution)/shard_map/jit(_solve_triangular)/triangular_solve | solution.py:17
  815.0 43.4 %all-reduce.29.cloned.1.call-done = f32[3,256,256]{1,2,0:T(8,128)} async-done(((f32[3,256,256]{1,2,0:T(8,128)}), f32[3,256,256]{1,2,0:T(8,128)}) %all-reduce.29.cloned.1.call-update) | async-done | bytes 786448 | tf_op jit(solution)/shard_map/psum | solution.py:11
  858.4 2.5 select_bitcast_fusion.2
  861.3 59.1 %all-reduce.33.cloned.1.call-done = (f32[3,1,256,256]{2,3,0,1:T(8,128)}, f32[3,1,256,256]{2,3,0,1:T(8,128)}) async-done(((f32[3,1,256,256]{2,3,0,1:T(8,128)}, f32[3,1,256,256]{2,3,0,1:T(8,128)}), (f32[3,1,256,256]{2,3,0,1:T(8,128)}, f32[3,1,256,256]{2,3,0,1:T(8,128)})) %all-reduce.33.cloned.1.call-update) | async-done | bytes 1572880 | tf_op jit(solution)/shard_map/psum | solution.py:11
  920.4 2.7 pad_maximum_fusion.2
  923.1 3.0 copy.47
  926.1 7.0 convolution_subtract_fusion
  933.1 2.2 copy-done
  935.2 2.2 copy.112
  937.5 1.2 fusion
  941.7 5.7 select_bitcast_fusion
  947.4 12.1 %copy.53 = f32[1,3,256,1,6,256]{5,3,4,2,1,0:T(1,128)} copy(f32[1,3,256,1,6,256]{2,5,4,1,3,0:T(8,128)} %select_bitcast_fusion) | data formatting | bytes 9437184
  959.5 149.2 %all-reduce.31.cloned.1.call-done = f32[1,3,256,6,256]{2,4,3,1,0:T(8,128)} async-done(((f32[1,3,256,6,256]{2,4,3,1,0:T(8,128)}), f32[1,3,256,6,256]{2,4,3,1,0:T(8,128)}) %all-reduce.31.cloned.1.call-update) | async-done | bytes 4718608 | tf_op jit(solution)/shard_map/psum | solution.py:68
  1108.7 6.0 copy.54
  (132 shorter events, 29.1 us)
Async XLA Ops:
  7.2 201.1 %all-reduce.17.cloned.1.call-start = ((), (), s32[]{:S(2)}) async-start(), calls=%async_computation | async-start | bytes 9437184 | tf_op jit(solution)/shard_map/psum | solution.py:44
  36.9 270.5 %all-reduce.19.cloned.1.call-start = ((), (), s32[]{:S(2)}) async-start(), calls=%async_computation.1 | async-start | bytes 524288 | tf_op jit(solution)/shard_map/psum | solution.py:11
  214.5 2.2 copy-start.1
  216.7 38.1 %slice-start = ((f32[3,256,6,256]{1,3,2,0:T(8,128)}), f32[3,256,1,256]{1,3,2,0:T(8,128)S(1)}, s32[]{:S(2)}) async-start(f32[3,256,6,256]{1,3,2,0:T(8,128)} %copy-done.1), calls=%async_computation.11 | async-start | bytes 1572864 | tf_op jit(solution)/shard_map/slice | solution.py:55
  254.4 124.9 %all-reduce.21.cloned.1.call-start = ((), (), s32[]{:S(2)}) async-start(), calls=%async_computation.2 | async-start | bytes 1572864 | tf_op jit(solution)/shard_map/psum | solution.py:11
  307.4 27.3 %copy-start.7 = (f32[256,256]{1,0:T(8,128)S(1)}, f32[256,256]{1,0:T(8,128)}, u32[]{:S(2)}) copy-start(f32[256,256]{1,0:T(8,128)} %all-reduce.19.cloned.1.call-done) | copy-start | bytes 786436
  335.8 105.4 %all-reduce.37.cloned.1.call-start = ((), (), s32[]{:S(2)}) async-start(), calls=%async_computation.10 | async-start | bytes 3145728 | tf_op jit(solution)/shard_map/psum | solution.py:11
  379.3 65.0 %copy-start.5 = (f32[3,256,256]{1,2,0:T(8,128)S(1)}, f32[3,256,256]{1,2,0:T(8,128)}, u32[]{:S(2)}) copy-start(f32[3,256,256]{1,2,0:T(8,128)} %all-reduce.21.cloned.1.call-done) | copy-start | bytes 2359300
  381.8 163.8 %all-reduce.23.cloned.1.call-start = ((), (), s32[]{:S(2)}) async-start(), calls=%async_computation.3 | async-start | bytes 524288 | tf_op jit(solution)/shard_map/psum | solution.py:11
  451.7 2.2 copy-start.2
  453.9 38.5 %slice-start.1 = ((f32[3,256,6,256]{1,3,2,0:T(8,128)}), f32[3,256,1,256]{1,3,2,0:T(8,128)S(1)}, s32[]{:S(2)}) async-start(f32[3,256,6,256]{1,3,2,0:T(8,128)} %copy-done.2), calls=%async_computation.12 | async-start | bytes 1572864 | tf_op jit(solution)/shard_map/slice | solution.py:55
  492.3 125.1 %all-reduce.25.cloned.1.call-start = ((), (), s32[]{:S(2)}) async-start(), calls=%async_computation.4 | async-start | bytes 1572864 | tf_op jit(solution)/shard_map/psum | solution.py:11
  545.6 27.2 %copy-start.9 = (f32[256,256]{1,0:T(8,128)S(1)}, f32[256,256]{1,0:T(8,128)}, u32[]{:S(2)}) copy-start(f32[256,256]{1,0:T(8,128)} %all-reduce.23.cloned.1.call-done) | copy-start | bytes 786436
  574.0 105.5 %all-reduce.35.cloned.1.call-start = ((), (), s32[]{:S(2)}) async-start(), calls=%async_computation.9 | async-start | bytes 3145728 | tf_op jit(solution)/shard_map/psum | solution.py:11
  617.4 67.8 %copy-start.4 = (f32[3,256,256]{1,2,0:T(8,128)S(1)}, f32[3,256,256]{1,2,0:T(8,128)}, u32[]{:S(2)}) copy-start(f32[3,256,256]{1,2,0:T(8,128)} %all-reduce.25.cloned.1.call-done) | copy-start | bytes 2359300
  619.9 166.7 %all-reduce.27.cloned.1.call-start = ((), (), s32[]{:S(2)}) async-start(), calls=%async_computation.5 | async-start | bytes 524288 | tf_op jit(solution)/shard_map/psum | solution.py:11
  692.6 2.2 copy-start.3
  694.8 38.6 %slice-start.2 = ((f32[3,256,6,256]{1,3,2,0:T(8,128)}), f32[3,256,1,256]{1,3,2,0:T(8,128)S(1)}, s32[]{:S(2)}) async-start(f32[3,256,6,256]{1,3,2,0:T(8,128)} %copy-done.3), calls=%async_computation.13 | async-start | bytes 1572864 | tf_op jit(solution)/shard_map/slice | solution.py:55
  733.3 125.1 %all-reduce.29.cloned.1.call-start = ((), (), s32[]{:S(2)}) async-start(), calls=%async_computation.6 | async-start | bytes 1572864 | tf_op jit(solution)/shard_map/psum | solution.py:11
  786.6 27.2 %copy-start.8 = (f32[256,256]{1,0:T(8,128)S(1)}, f32[256,256]{1,0:T(8,128)}, u32[]{:S(2)}) copy-start(f32[256,256]{1,0:T(8,128)} %all-reduce.27.cloned.1.call-done) | copy-start | bytes 786436
  815.0 105.4 %all-reduce.33.cloned.1.call-start = ((), (), s32[]{:S(2)}) async-start(), calls=%async_computation.8 | async-start | bytes 3145728 | tf_op jit(solution)/shard_map/psum | solution.py:11
  858.4 67.7 %copy-start.6 = (f32[3,256,256]{1,2,0:T(8,128)S(1)}, f32[3,256,256]{1,2,0:T(8,128)}, u32[]{:S(2)}) copy-start(f32[3,256,256]{1,2,0:T(8,128)} %all-reduce.29.cloned.1.call-done) | copy-start | bytes 2359300
  860.9 247.8 %all-reduce.31.cloned.1.call-start = ((), (), s32[]{:S(2)}) async-start(), calls=%async_computation.7 | async-start | bytes 9437184 | tf_op jit(solution)/shard_map/psum | solution.py:68
  933.1 2.2 copy-start
Sparse Core Ops, SparseCore 0:
  37.0 171.1 all-reduce.16
  254.5 52.8 all-reduce.18
  336.0 43.2 all-reduce.20
  383.0 58.2 all-reduce.36
  492.4 53.0 all-reduce.22
  574.1 43.2 all-reduce.24
  621.2 58.2 all-reduce.34
  733.4 53.0 all-reduce.26
  815.1 43.2 all-reduce.28
  862.1 58.2 all-reduce.32
  937.6 171.1 all-reduce.30
where the time goes:
time: 1130 us; the launch traced here: 1120 us
  waiting for transfers between devices  780 us (69%)
  other arithmetic  209 us (18%)
  local copies, waits for them, and re-layouts  72.9 us (6%)
  matrix products  28.6 us (3%)
  between operations  19.4 us (2%)
    psum x9, waiting for transfers between devices, spread_2(): return lax.psum(block, axis)  466 us
    psum x1, waiting for transfers between devices, shards(): remaining_peers = lax.psum(healthy_member, 'col')  165 us
    psum x1, waiting for transfers between devices, shards(): totals = lax.psum(work, 'col')  149 us
    another operation x20, other arithmetic, shards(): factor_here = jnp.linalg.cholesky(diag_input)  103 us
    another operation x7, other arithmetic, solve_panel(): jax.scipy.linalg.solve_triangular(factor, stacked.T, lower=True)  62.1 us
    unnamed x28, local copies, waits for them, and re-layouts  49.2 us
  transfers between devices with their start and end apart: 11, of which 11 were waited for; matrix products, arithmetic and copies ran while one was open for 3% of the time, Pallas kernels for 0%

commit v1 on v0

--- a/solution.py
+++ b/solution.py
@@ -41,7 +41,17 @@
     totals = checksum.reshape(tile_rows, width, tile_cols, width)
     missing_tiles = lax.all_gather(failed, "col", axis=0, tiled=True)[0]
     healthy_member = jnp.where(column_position != missing_tiles, resident_tiles, 0.0)
-    remaining_peers = lax.psum(healthy_member, "col")
+
+    def put_works(x_in, peer_axis):
+        extent = lax.axis_size(peer_axis)
+        high = lambda main: [(rr, rr ^ main) for rr in range(extent)]
+        p_next = x_in
+        for k0 in range(extent.bit_length() - 1):
+            placed = lax.ppermute(p_next, peer_axis, high(1 << k0))
+            p_next = p_next + placed
+        return p_next
+
+    remaining_peers = put_works(healthy_member, "col")
     work = jnp.where(column_position == missing_tiles, totals - remaining_peers, resident_tiles)
     row_tiles = row_index + jnp.arange(tile_rows, dtype=jnp.int32) * rows_count
     col_tiles = column_position + jnp.arange(tile_cols, dtype=jnp.int32) * cols_count

time: 1130 us -> 1270 us (1.12)
  waiting for transfers between devices: 780 us -> 912 us
    ppermute x0 -> x2, waiting for transfers between devices: none -> 297 us  [put_works(): placed = lax.ppermute(p_next, peer_axis, high(1 << k0))]
    psum x1 -> x0, waiting for transfers between devices: 165 us -> none  [shards(): remaining_peers = lax.psum(healthy_member, 'col')]
    unnamed x28 -> x30, local copies, waits for them, and re-layouts: 49.2 us -> 49.2 us
  transfers between devices with their start and end apart: 11 -> 12, of which waited for: 11 -> 12; matrix products, arithmetic and copies ran while one was open for 3% -> 2% of each run, Pallas kernels for 0% -> 0%
where the time goes in v1:
time: 1270 us; the launch traced here: 1260 us
  waiting for transfers between devices  912 us (72%)
  other arithmetic  211 us (17%)
  local copies, waits for them, and re-layouts  73.2 us (6%)
  matrix products  28.6 us (2%)
  between operations  20.1 us (2%)
    psum x9, waiting for transfers between devices, spread_2(): return lax.psum(block, axis)  466 us
    ppermute x2, waiting for transfers between devices, put_works(): placed = lax.ppermute(p_next, peer_axis, high(1 << k0))  297 us
    psum x1, waiting for transfers between devices, shards(): totals = lax.psum(work, 'col')  149 us
    another operation x20, other arithmetic, shards(): factor_here = jnp.linalg.cholesky(diag_input)  104 us
    another operation x7, other arithmetic, solve_panel(): jax.scipy.linalg.solve_triangular(factor, stacked.T, lower=True)  62.1 us
    unnamed x30, local copies, waits for them, and re-layouts  49.2 us
  transfers between devices with their start and end apart: 12, of which 12 were waited for; matrix products, arithmetic and copies ran while one was open for 2% of the time, Pallas kernels for 0%

profile of v1, /device:TPU:0, one launch (start us, length us, event | category | flops | bytes accessed | tf_op | source)
XLA Modules:
  0.0 1258.5 jit_solution(13722917386310519270)
XLA Ops:
  7.9 1.2 dynamic-slice.31
  9.9 9.9 all-reduce.1
  19.8 12.1 copy.25
  31.9 2.9 bitcast_select_fusion.1
  34.8 1.6 collective-permute-start
  36.5 99.9 %collective-permute-done = f32[3,256,6,256]{1,3,2,0:T(8,128)S(1)} collective-permute-done((f32[3,256,6,256]{1,3,2,0:T(8,128)S(1)}, f32[3,256,6,256]{1,3,2,0:T(8,128)S(1)}, u32[]{:S(2)}, u32[]{:S(2)}) %collective-permute-start) | collective-permute-done | bytes 4718624 | tf_op jit(solution)/shard_map/ppermute | solution.py:50
  136.4 2.7 fusion.49
  139.4 6.0 copy.24
  145.5 196.7 %collective-permute-done.1 = f32[3,256,6,256]{1,3,2,0:T(8,128)} collective-permute-done((f32[3,256,6,256]{1,3,2,0:T(8,128)}, f32[3,256,6,256]{1,3,2,0:T(8,128)}, u32[]{:S(2)}, u32[]{:S(2)}) %collective-permute-start.1) | collective-permute-done | bytes 4718624 | tf_op jit(solution)/shard_map/ppermute | solution.py:50
  342.2 7.8 bitcast_select_fusion
  350.0 2.2 copy-done.2
  352.3 1.1 fusion.13
  353.4 11.7 cholesky.172
  365.2 9.8 custom-call.15
  375.5 11.7 cholesky.189
  390.7 52.2 %all-reduce.16.cloned.1.call-done = f32[256,256]{1,0:T(8,128)} async-done(((f32[256,256]{1,0:T(8,128)}), f32[256,256]{1,0:T(8,128)}) %all-reduce.16.cloned.1.call-update) | async-done | bytes 262160 | tf_op jit(solution)/shard_map/psum | solution.py:11
  444.1 4.1 while.9
  444.7 1.4 bitcast_dynamic-update-slice_fusion.9
  446.8 1.4 bitcast_dynamic-update-slice_fusion.9
  448.2 19.7 %custom-call.16 = f32[2,128,128]{1,2,0:T(8,128)S(1)} custom-call(f32[2,128,128]{2,1,0:T(8,128)S(1)} %get-tuple-element.60), custom_call_target="InvertDiagBlocksLowerTriangular" | custom-call | tf_op jit(solution)/shard_map/jit(_solve_triangular)/triangular_solve | solution.py:17
  471.6 43.3 %all-reduce.18.cloned.1.call-done = f32[3,256,256]{1,2,0:T(8,128)} async-done(((f32[3,256,256]{1,2,0:T(8,128)}), f32[3,256,256]{1,2,0:T(8,128)}) %all-reduce.18.cloned.1.call-update) | async-done | bytes 786448 | tf_op jit(solution)/shard_map/psum | solution.py:11
  515.0 2.5 select_bitcast_fusion.6
  517.6 59.5 %all-reduce.34.cloned.1.call-done = (f32[3,1,256,256]{2,3,0,1:T(8,128)}, f32[3,1,256,256]{2,3,0,1:T(8,128)}) async-done(((f32[3,1,256,256]{2,3,0,1:T(8,128)}, f32[3,1,256,256]{2,3,0,1:T(8,128)}), (f32[3,1,256,256]{2,3,0,1:T(8,128)}, f32[3,1,256,256]{2,3,0,1:T(8,128)})) %all-reduce.34.cloned.1.call-update) | async-done | bytes 1572880 | tf_op jit(solution)/shard_map/psum | solution.py:11
  577.1 1.5 pad_maximum_fusion
  578.6 1.6 copy.31
  580.2 7.3 convolution_subtract_fusion.2
  587.6 2.2 copy-done.3
  589.9 1.1 fusion.12
  591.0 11.7 cholesky.206
  602.8 9.8 custom-call.17
  613.1 11.9 cholesky.223
  628.8 52.9 %all-reduce.20.cloned.1.call-done = f32[256,256]{1,0:T(8,128)} async-done(((f32[256,256]{1,0:T(8,128)}), f32[256,256]{1,0:T(8,128)}) %all-reduce.20.cloned.1.call-update) | async-done | bytes 262160 | tf_op jit(solution)/shard_map/psum | solution.py:11
  682.7 4.1 while.10
  683.4 1.4 bitcast_dynamic-update-slice_fusion.10
  685.4 1.4 bitcast_dynamic-update-slice_fusion.10
  686.9 19.7 %custom-call.18 = f32[2,128,128]{1,2,0:T(8,128)S(1)} custom-call(f32[2,128,128]{2,1,0:T(8,128)S(1)} %get-tuple-element.61), custom_call_target="InvertDiagBlocksLowerTriangular" | custom-call | tf_op jit(solution)/shard_map/jit(_solve_triangular)/triangular_solve | solution.py:17
  710.3 43.4 %all-reduce.22.cloned.1.call-done = f32[3,256,256]{1,2,0:T(8,128)} async-done(((f32[3,256,256]{1,2,0:T(8,128)}), f32[3,256,256]{1,2,0:T(8,128)}) %all-reduce.22.cloned.1.call-update) | async-done | bytes 786448 | tf_op jit(solution)/shard_map/psum | solution.py:11
  753.6 2.5 select_bitcast_fusion.4
  756.4 59.2 %all-reduce.32.cloned.1.call-done = (f32[3,1,256,256]{2,3,0,1:T(8,128)}, f32[3,1,256,256]{2,3,0,1:T(8,128)}) async-done(((f32[3,1,256,256]{2,3,0,1:T(8,128)}, f32[3,1,256,256]{2,3,0,1:T(8,128)}), (f32[3,1,256,256]{2,3,0,1:T(8,128)}, f32[3,1,256,256]{2,3,0,1:T(8,128)})) %all-reduce.32.cloned.1.call-update) | async-done | bytes 1572880 | tf_op jit(solution)/shard_map/psum | solution.py:11
  815.6 2.7 pad_maximum_fusion.1
  818.3 3.0 copy.39
  821.3 7.3 convolution_subtract_fusion.1
  828.7 2.2 copy-done.4
  832.1 11.7 cholesky.240
  843.9 9.8 custom-call.19
  854.2 12.0 cholesky.257
  869.9 52.9 %all-reduce.24.cloned.1.call-done = f32[256,256]{1,0:T(8,128)} async-done(((f32[256,256]{1,0:T(8,128)}), f32[256,256]{1,0:T(8,128)}) %all-reduce.24.cloned.1.call-update) | async-done | bytes 262160 | tf_op jit(solution)/shard_map/psum | solution.py:11
  923.9 4.0 while.11
  924.5 1.4 bitcast_dynamic-update-slice_fusion.11
  926.5 1.4 bitcast_dynamic-update-slice_fusion.11
  927.9 19.7 %custom-call.20 = f32[2,128,128]{1,2,0:T(8,128)S(1)} custom-call(f32[2,128,128]{2,1,0:T(8,128)S(1)} %get-tuple-element.62), custom_call_target="InvertDiagBlocksLowerTriangular" | custom-call | tf_op jit(solution)/shard_map/jit(_solve_triangular)/triangular_solve | solution.py:17
  951.3 43.4 %all-reduce.26.cloned.1.call-done = f32[3,256,256]{1,2,0:T(8,128)} async-done(((f32[3,256,256]{1,2,0:T(8,128)}), f32[3,256,256]{1,2,0:T(8,128)}) %all-reduce.26.cloned.1.call-update) | async-done | bytes 786448 | tf_op jit(solution)/shard_map/psum | solution.py:11
  994.7 2.5 select_bitcast_fusion.2
  997.5 59.3 %all-reduce.30.cloned.1.call-done = (f32[3,1,256,256]{2,3,0,1:T(8,128)}, f32[3,1,256,256]{2,3,0,1:T(8,128)}) async-done(((f32[3,1,256,256]{2,3,0,1:T(8,128)}, f32[3,1,256,256]{2,3,0,1:T(8,128)}), (f32[3,1,256,256]{2,3,0,1:T(8,128)}, f32[3,1,256,256]{2,3,0,1:T(8,128)})) %all-reduce.30.cloned.1.call-update) | async-done | bytes 1572880 | tf_op jit(solution)/shard_map/psum | solution.py:11
  1056.8 2.7 pad_maximum_fusion.2
  1059.5 3.0 copy.47
  1062.5 7.0 convolution_subtract_fusion
  1069.5 2.2 copy-done.1
  1071.6 2.2 copy.111
  1073.9 1.2 fusion
  1078.1 5.7 select_bitcast_fusion
  1083.8 12.1 copy.53
  1095.9 149.2 %all-reduce.28.cloned.1.call-done = f32[1,3,256,6,256]{2,4,3,1,0:T(8,128)} async-done(((f32[1,3,256,6,256]{2,4,3,1,0:T(8,128)}), f32[1,3,256,6,256]{2,4,3,1,0:T(8,128)}) %all-reduce.28.cloned.1.call-update) | async-done | bytes 4718608 | tf_op jit(solution)/shard_map/psum | solution.py:78
  1245.2 6.0 copy.54
  (136 shorter events, 32.7 us)
Async XLA Ops:
  7.2 435.8 %all-reduce.16.cloned.1.call-start = ((), (), s32[]{:S(2)}) async-start(), calls=%async_computation | async-start | bytes 524288 | tf_op jit(solution)/shard_map/psum | solution.py:11
  31.9 104.5 %copy-start = (f32[1,3,256,1,6,256]{2,5,4,1,3,0:T(8,128)S(1)}, f32[1,3,256,1,6,256]{2,5,4,1,3,0:T(8,128)}, u32[]{:S(2)}) copy-start(f32[1,3,256,1,6,256]{2,5,4,1,3,0:T(8,128)} %copy.25) | copy-start | bytes 14155780
  34.8 101.6 %collective-permute-start = (f32[3,256,6,256]{1,3,2,0:T(8,128)S(1)}, f32[3,256,6,256]{1,3,2,0:T(8,128)S(1)}, u32[]{:S(2)}, u32[]{:S(2)}) collective-permute-start(f32[3,256,6,256]{1,3,2,0:T(8,128)S(1)} %bitcast_select_fusion.1), channel_id=1, source_target_pairs={{0,1},{1,0},{2,3},{3,2},{4,5},{5,4},{6,7},{7,6},{8,9},{9,8},{10,11... | collective-permute-start | bytes 14155784 | tf_op jit(solution)/shard_map/ppermute | solution.py:50
  139.2 203.0 %collective-permute-start.1 = (f32[3,256,6,256]{1,3,2,0:T(8,128)}, f32[3,256,6,256]{1,3,2,0:T(8,128)}, u32[]{:S(2)}, u32[]{:S(2)}) collective-permute-start(f32[3,256,6,256]{1,3,2,0:T(8,128)} %fusion.49), channel_id=1, source_target_pairs={{0,2},{1,3},{2,0},{3,1},{4,6},{5,7},{6,4},{7,5},{8,10},{9,11},{10,... | collective-permute-start | bytes 14155784 | tf_op jit(solution)/shard_map/ppermute | solution.py:50
  350.0 2.2 copy-start.2
  352.2 38.3 %slice-start = ((f32[3,256,6,256]{1,3,2,0:T(8,128)}), f32[3,256,1,256]{1,3,2,0:T(8,128)S(1)}, s32[]{:S(2)}) async-start(f32[3,256,6,256]{1,3,2,0:T(8,128)} %copy-done.2), calls=%async_computation.10 | async-start | bytes 1572864 | tf_op jit(solution)/shard_map/slice | solution.py:65
  390.0 124.9 %all-reduce.18.cloned.1.call-start = ((), (), s32[]{:S(2)}) async-start(), calls=%async_computation.1 | async-start | bytes 1572864 | tf_op jit(solution)/shard_map/psum | solution.py:11
  443.0 27.4 %copy-start.8 = (f32[256,256]{1,0:T(8,128)S(1)}, f32[256,256]{1,0:T(8,128)}, u32[]{:S(2)}) copy-start(f32[256,256]{1,0:T(8,128)} %all-reduce.16.cloned.1.call-done) | copy-start | bytes 786436
  471.6 105.5 %all-reduce.34.cloned.1.call-start = ((), (), s32[]{:S(2)}) async-start(), calls=%async_computation.9 | async-start | bytes 3145728 | tf_op jit(solution)/shard_map/psum | solution.py:11
  515.0 65.2 %copy-start.6 = (f32[3,256,256]{1,2,0:T(8,128)S(1)}, f32[3,256,256]{1,2,0:T(8,128)}, u32[]{:S(2)}) copy-start(f32[3,256,256]{1,2,0:T(8,128)} %all-reduce.18.cloned.1.call-done) | copy-start | bytes 2359300
  517.5 164.2 %all-reduce.20.cloned.1.call-start = ((), (), s32[]{:S(2)}) async-start(), calls=%async_computation.2 | async-start | bytes 524288 | tf_op jit(solution)/shard_map/psum | solution.py:11
  587.5 2.2 copy-start.3
  589.8 38.7 %slice-start.1 = ((f32[3,256,6,256]{1,3,2,0:T(8,128)}), f32[3,256,1,256]{1,3,2,0:T(8,128)S(1)}, s32[]{:S(2)}) async-start(f32[3,256,6,256]{1,3,2,0:T(8,128)} %copy-done.3), calls=%async_computation.11 | async-start | bytes 1572864 | tf_op jit(solution)/shard_map/slice | solution.py:65
  628.4 125.2 %all-reduce.22.cloned.1.call-start = ((), (), s32[]{:S(2)}) async-start(), calls=%async_computation.3 | async-start | bytes 1572864 | tf_op jit(solution)/shard_map/psum | solution.py:11
  681.7 27.3 %copy-start.10 = (f32[256,256]{1,0:T(8,128)S(1)}, f32[256,256]{1,0:T(8,128)}, u32[]{:S(2)}) copy-start(f32[256,256]{1,0:T(8,128)} %all-reduce.20.cloned.1.call-done) | copy-start | bytes 786436
  710.2 105.4 %all-reduce.32.cloned.1.call-start = ((), (), s32[]{:S(2)}) async-start(), calls=%async_computation.8 | async-start | bytes 3145728 | tf_op jit(solution)/shard_map/psum | solution.py:11
  753.6 67.7 %copy-start.5 = (f32[3,256,256]{1,2,0:T(8,128)S(1)}, f32[3,256,256]{1,2,0:T(8,128)}, u32[]{:S(2)}) copy-start(f32[3,256,256]{1,2,0:T(8,128)} %all-reduce.22.cloned.1.call-done) | copy-start | bytes 2359300
  756.1 166.7 %all-reduce.24.cloned.1.call-start = ((), (), s32[]{:S(2)}) async-start(), calls=%async_computation.4 | async-start | bytes 524288 | tf_op jit(solution)/shard_map/psum | solution.py:11
  828.6 2.2 copy-start.4
  830.9 38.8 %slice-start.2 = ((f32[3,256,6,256]{1,3,2,0:T(8,128)}), f32[3,256,1,256]{1,3,2,0:T(8,128)S(1)}, s32[]{:S(2)}) async-start(f32[3,256,6,256]{1,3,2,0:T(8,128)} %copy-done.4), calls=%async_computation.12 | async-start | bytes 1572864 | tf_op jit(solution)/shard_map/slice | solution.py:65
  869.6 125.1 %all-reduce.26.cloned.1.call-start = ((), (), s32[]{:S(2)}) async-start(), calls=%async_computation.5 | async-start | bytes 1572864 | tf_op jit(solution)/shard_map/psum | solution.py:11
  922.9 27.2 %copy-start.9 = (f32[256,256]{1,0:T(8,128)S(1)}, f32[256,256]{1,0:T(8,128)}, u32[]{:S(2)}) copy-start(f32[256,256]{1,0:T(8,128)} %all-reduce.24.cloned.1.call-done) | copy-start | bytes 786436
  951.2 105.5 %all-reduce.30.cloned.1.call-start = ((), (), s32[]{:S(2)}) async-start(), calls=%async_computation.7 | async-start | bytes 3145728 | tf_op jit(solution)/shard_map/psum | solution.py:11
  994.7 67.8 %copy-start.7 = (f32[3,256,256]{1,2,0:T(8,128)S(1)}, f32[3,256,256]{1,2,0:T(8,128)}, u32[]{:S(2)}) copy-start(f32[3,256,256]{1,2,0:T(8,128)} %all-reduce.26.cloned.1.call-done) | copy-start | bytes 2359300
  997.2 248.0 %all-reduce.28.cloned.1.call-start = ((), (), s32[]{:S(2)}) async-start(), calls=%async_computation.6 | async-start | bytes 9437184 | tf_op jit(solution)/shard_map/psum | solution.py:78
  1069.5 2.2 copy-start.1
Sparse Core Ops, SparseCore 0:
  390.2 52.7 all-reduce.15
  471.7 43.2 all-reduce.17
  518.9 58.2 all-reduce.33
  628.5 53.0 all-reduce.19
  710.3 43.2 all-reduce.21
  757.3 58.2 all-reduce.31
  869.7 53.0 all-reduce.23
  951.4 43.2 all-reduce.25
  998.5 58.2 all-reduce.29
  1074.0 171.1 all-reduce.27
